TPU v7x, 768 devices: a whole 4x8x12 slice. The times are simulated.
768 devices in a mesh: batch: 192 (over x, y, z_lo), seq: 4 (over z_hi, core).
Axes of the slice: x: 4, y: 8, z: 12 (z_hi: 2, z_lo: 6; z = z_hi * 6 + z_lo), core: 2. Of those that a mesh axis runs over, the one named last changes fastest.
Arguments:
- track_input: bfloat16 [294912, 768], P(('batch', 'seq')), parts along dimension 0, may hold values from -6 to 6
- conv_gain: float32 [4, 768], replicated, may hold values from 0.1 to 1.9
- conv_kernel: float32 [4, 5, 768], replicated, may hold values from -3 to 3
- dilation: int32 [4], replicated, may hold values from 1 to 8, as said below
- attn_gain: float32 [768], replicated, may hold values from 0.1 to 1.9
- w_qkv: bfloat16 [768, 2304], replicated, as said below
- w_out: bfloat16 [768, 768], replicated, may hold values from -1.75 to 1.75
- w_pair_a: bfloat16 [768, 512], replicated, may hold values from -0.21875 to 0.21875
- w_pair_b: bfloat16 [768, 512], replicated, may hold values from -0.21875 to 0.21875
Outputs:
- track_out: bfloat16 [294912, 768], P(('batch', 'seq')), parts along dimension 0
- pair_map: bfloat16 [12288, 96, 96], P('batch', 'seq'), parts along dimension 0
There are 192 independent parts, one for each index of `batch`. A program takes and returns all parts, laid end to end along the dimension named above; an argument that names none is the same for every part. Nothing has to cross between parts.
Inputs may be any that keep to these rules, and one draw needn't show every extreme that they name: Every dilation lies in 1 to 8; exactly one layer has dilation 8, the others less. `w_qkv`: a projection matrix with entries of order 768^-0.5 or larger.
All inputs are finite; a program needn't handle non-finite values.
Results may differ from a plain program's by a relative error of at most 0.019.
The roundings to bfloat16 on the way count: a program that leaves them out, or rounds other values in their place, can miss the bound.
Values may be sent and summed in bfloat16 or wider, within the bound.
A program may use at most 64 MiB of HBM per device.

v0:
```python
import math

import jax
import jax.numpy as jnp
from jax import lax
from jax.sharding import PartitionSpec as P

HEADS = 8
KSIZE = 5
DMAX = 8
LAYERS = 4
POOL = 16
PCH = 64
R = 8


def with_halo(block, sides, width):
    for axis, dim in sides:
        count = lax.axis_size(axis)
        forward = [(i, i + 1) for i in range(count - 1)]
        backward = [(target, source) for source, target in forward]
        low = lax.ppermute(
            lax.slice_in_dim(block, block.shape[dim] - width, None, axis=dim), axis, forward
        )
        high = lax.ppermute(lax.slice_in_dim(block, 0, width, axis=dim), axis, backward)
        block = jnp.concatenate([low, block, high], axis=dim)
    return block


def rms_norm(values, gain):
    return values * lax.rsqrt(jnp.mean(values * values, axis=-1, keepdims=True) + 1e-06) * gain


def dilated_conv(padded, norm_gain, kernel, dilation_rate, out_len):
    rim_width = KSIZE // 2 * DMAX
    normed = rms_norm(padded, norm_gain)
    total = jnp.zeros((out_len, padded.shape[1]), jnp.float32)
    for tap_index in range(KSIZE):
        start = rim_width + (tap_index - KSIZE // 2) * dilation_rate
        total = total + kernel[tap_index] * lax.dynamic_slice_in_dim(normed, start, out_len, 0)
    return padded[rim_width : rim_width + out_len] + jax.nn.gelu(total)


def body(
    track_input, conv_gain, conv_kernel, dilation, attn_gain, w_qkv, w_out, w_pair_a, w_pair_b
):
    row_count = track_input.shape[0]
    feature_count = track_input.shape[1]
    head_size = feature_count // HEADS
    rim_width = KSIZE // 2 * DMAX
    layer_state = track_input.astype(jnp.float32)
    for layer in range(LAYERS):
        padded = with_halo(layer_state, (("seq", 0),), rim_width)
        layer_state = dilated_conv(
            padded, conv_gain[layer], conv_kernel[layer], dilation[layer], row_count
        )
    normed = rms_norm(layer_state, attn_gain).astype(jnp.bfloat16)
    projected = jnp.dot(normed, w_qkv, preferred_element_type=jnp.float32).astype(jnp.bfloat16)
    queries = projected[:, :feature_count]
    key_rows = projected[:, feature_count : 2 * feature_count]
    value_rows = projected[:, 2 * feature_count :]
    query_heads = queries.reshape(row_count, HEADS, head_size).transpose(1, 0, 2)
    initial = (
        jnp.full((HEADS, row_count), -1e30, jnp.float32),
        jnp.zeros((HEADS, row_count), jnp.float32),
        jnp.zeros((HEADS, row_count, head_size), jnp.float32),
    )
    piece_keys = lax.all_gather(key_rows, "seq", axis=0, tiled=True)
    piece_values = lax.all_gather(value_rows, "seq", axis=0, tiled=True)
    count = piece_keys.shape[0]
    key_heads = piece_keys.reshape(count, HEADS, head_size).transpose(1, 0, 2)
    value_heads = piece_values.reshape(count, HEADS, head_size).transpose(1, 0, 2)

    def per_head(operands):
        running_max, running_sum, running_acc, query_head, key_head, value_head = operands
        scores = jnp.dot(query_head, key_head.T, preferred_element_type=jnp.float32) / math.sqrt(
            head_size
        )
        new_max = jnp.maximum(running_max, scores.max(axis=1))
        rescale = jnp.exp(running_max - new_max)
        probs = jnp.exp(scores - new_max[:, None])
        new_sum = running_sum * rescale + probs.sum(axis=1)
        new_acc = running_acc * rescale[:, None] + jnp.dot(
            probs.astype(jnp.bfloat16), value_head, preferred_element_type=jnp.float32
        )
        return (new_max, new_sum, new_acc)

    final_max, final_sum, final_acc = lax.map(
        per_head, (initial[0], initial[1], initial[2], query_heads, key_heads, value_heads)
    )
    mixed = (
        (final_acc / final_sum[:, :, None])
        .transpose(1, 0, 2)
        .reshape(row_count, feature_count)
        .astype(jnp.bfloat16)
    )
    output = layer_state + jnp.dot(mixed, w_out, preferred_element_type=jnp.float32)
    track_out = output.astype(jnp.bfloat16)
    pooled = rms_norm(
        output.reshape(row_count // POOL, POOL, feature_count).mean(axis=1), 1.0
    ).astype(jnp.bfloat16)
    left_side = (
        jnp.dot(pooled, w_pair_a, preferred_element_type=jnp.float32)
        .astype(jnp.bfloat16)
        .reshape(row_count // POOL, R, PCH)
    )
    right_local = jnp.dot(pooled, w_pair_b, preferred_element_type=jnp.float32).astype(jnp.bfloat16)
    piece = lax.all_gather(right_local, "seq", axis=0, tiled=True)
    right_side = piece.reshape(piece.shape[0], R, PCH)
    product = jnp.einsum("irc,jrc->cij", left_side, right_side, preferred_element_type=jnp.float32)
    pair_map = (product / math.sqrt(R)).astype(jnp.bfloat16)
    return (track_out, pair_map)


def solution(mesh):
    placed = (P(("batch", "seq"), None), P(), P(), P(), P(), P(), P(), P(), P())
    return jax.shard_map(
        body,
        mesh=mesh,
        in_specs=placed,
        out_specs=(P(("batch", "seq"), None), P("batch", "seq", None)),
        check_vma=False,
    )
```

profile of v0, /device:TPU:1, one launch (start us, length us, event | category | flops | bytes accessed | tf_op | source)
XLA Modules:
  0.0 337.2 jit_solution(11118549796613187937)
XLA Ops:
  8.8 12.4 %collective-permute-start.1 = (f32[16,768]{1,0:T(8,128)}, f32[16,768]{1,0:T(8,128)}, u32[]{:S(2)}, u32[]{:S(2)}) collective-permute-start(f32[16,768]{1,0:T(8,128)} %get-tuple-element.100), channel_id=1, source_target_pairs={{1,0},{2,1},{3,2},{5,4},{6,5},{7,6},{9,8},{10,9},{11,10},{13,12},{... | collective-permute-start | bytes 147464 | tf_op jit(solution)/shard_map/ppermute | solution.py:25
  21.2 5.7 %collective-permute-start = (f32[16,768]{1,0:T(8,128)}, f32[16,768]{1,0:T(8,128)}, u32[]{:S(2)}, u32[]{:S(2)}) collective-permute-start(f32[16,768]{1,0:T(8,128)} %get-tuple-element.99), channel_id=1, source_target_pairs={{0,1},{1,2},{2,3},{4,5},{5,6},{6,7},{8,9},{9,10},{10,11},{12,13},{... | collective-permute-start | bytes 147464 | tf_op jit(solution)/shard_map/ppermute | solution.py:22
  31.7 2.1 convert_element_type.36
  44.1 10.0 %collective-permute-start.2 = (f32[16,768]{1,0:T(8,128)}, f32[16,768]{1,0:T(8,128)}, u32[]{:S(2)}, u32[]{:S(2)}) collective-permute-start(f32[16,768]{1,0:T(8,128)} %get-tuple-element.97), channel_id=1, source_target_pairs={{0,1},{1,2},{2,3},{4,5},{5,6},{6,7},{8,9},{9,10},{10,11},{12,13},{... | collective-permute-start | bytes 147464 | tf_op jit(solution)/shard_map/ppermute | solution.py:22
  64.7 10.0 %collective-permute-start.4 = (f32[16,768]{1,0:T(8,128)}, f32[16,768]{1,0:T(8,128)}, u32[]{:S(2)}, u32[]{:S(2)}) collective-permute-start(f32[16,768]{1,0:T(8,128)} %get-tuple-element.95), channel_id=1, source_target_pairs={{0,1},{1,2},{2,3},{4,5},{5,6},{6,7},{8,9},{9,10},{10,11},{12,13},{... | collective-permute-start | bytes 147464 | tf_op jit(solution)/shard_map/ppermute | solution.py:22
  85.3 10.0 %collective-permute-start.6 = (f32[16,768]{1,0:T(8,128)}, f32[16,768]{1,0:T(8,128)}, u32[]{:S(2)}, u32[]{:S(2)}) collective-permute-start(f32[16,768]{1,0:T(8,128)} %get-tuple-element.93), channel_id=1, source_target_pairs={{0,1},{1,2},{2,3},{4,5},{5,6},{6,7},{8,9},{9,10},{10,11},{12,13},{... | collective-permute-start | bytes 147464 | tf_op jit(solution)/shard_map/ppermute | solution.py:22
  107.6 2.1 copy.25
  109.7 63.7 %all-gather.3.cloned.1.call-done = bf16[1536,768]{1,0:T(8,128)(2,1)} async-done(((bf16[384,768]{1,0:T(8,128)(2,1)}), bf16[1536,768]{1,0:T(8,128)(2,1)}) %all-gather.3.cloned.1.call-update) | async-done | bytes 2359312 | tf_op jit(solution)/shard_map/all_gather | solution.py:68
  173.4 4.3 %copy.26 = bf16[1536,768]{0,1:T(8,128)(2,1)} copy(bf16[1536,768]{1,0:T(8,128)(2,1)} %all-gather.3.cloned.1.call-done) | data formatting | bytes 4718592 | tf_op jit(solution)/shard_map/all_gather | solution.py:68
  177.7 59.7 %all-gather.5.cloned.1.call-done = bf16[1536,768]{1,0:T(8,128)(2,1)} async-done(((bf16[384,768]{1,0:T(8,128)(2,1)}), bf16[1536,768]{1,0:T(8,128)(2,1)}) %all-gather.5.cloned.1.call-update) | async-done | bytes 2359312 | tf_op jit(solution)/shard_map/all_gather | solution.py:69
  237.3 4.3 %copy.27 = bf16[1536,768]{0,1:T(8,128)(2,1)} copy(bf16[1536,768]{1,0:T(8,128)(2,1)} %all-gather.5.cloned.1.call-done) | data formatting | bytes 4718592 | tf_op jit(solution)/shard_map/all_gather | solution.py:69
  241.6 58.4 %while.12 = (s32[]{:T(128)}, f32[8,384]{1,0:T(8,128)}, f32[8,384,96]{1,2,0:T(8,128)}, bf16[8,384,96]{1,2,0:T(8,128)(2,1)}, bf16[8,1536,96]{1,2,0:T(8,128)(2,1)},...) while((s32[]{:T(128)}, f32[8,384]{1,0:T(8,128)}, f32[8,384,96]{1,2,0:T(8,128)}, ...), condition=%wide.region_8.9_spmd, body=%wide.region_5.8_spmd.sunk | while | flops 230069376 | bytes 17351292 | solution.py:88
  246.0 3.0 fusion.95
  253.3 2.9 fusion.95
  260.6 2.9 fusion.95
  267.9 2.9 fusion.95
  275.2 2.9 fusion.95
  282.5 2.9 fusion.95
  289.7 2.9 fusion.95
  297.0 2.9 fusion.95
  301.6 3.1 fusion.79
  304.8 2.1 reduce_sum.79
  314.4 12.2 %all_gather.11 = bf16[96,512]{1,0:T(8,128)(2,1)} all-gather(bf16[24,512]{1,0:T(8,128)(2,1)S(1)} %convolution_convert_fusion.1), channel_id=1, replica_groups=mesh['batch'=192,'seq'=4] {'seq'}, dimensions={0}, use_global_device_ids=true | all-gather | bytes 122880 | tf_op jit(solution)/shard_map/all_gather | solution.py:108
  328.2 2.1 fusion.23
  (180 shorter events, 82.9 us)
Async XLA Ops:
  7.2 96.8 %copy-start = (bf16[768,2304]{1,0:T(8,128)(2,1)S(1)}, bf16[768,2304]{1,0:T(8,128)(2,1)}, u32[]{:S(2)}) copy-start(bf16[768,2304]{1,0:T(8,128)(2,1)} %param.16) | copy-start | bytes 10616836
  7.2 166.2 %all-gather.3.cloned.1.call-start = ((), (), s32[]{:S(2)}) async-start(), calls=%async_computation | async-start | bytes 2949120 | tf_op jit(solution)/shard_map/all_gather | solution.py:68
  8.8 27.8 %collective-permute-start.1 = (f32[16,768]{1,0:T(8,128)}, f32[16,768]{1,0:T(8,128)}, u32[]{:S(2)}, u32[]{:S(2)}) collective-permute-start(f32[16,768]{1,0:T(8,128)} %get-tuple-element.100), channel_id=1, source_target_pairs={{1,0},{2,1},{3,2},{5,4},{6,5},{7,6},{9,8},{10,9},{11,10},{13,12},{... | collective-permute-start | bytes 147464 | tf_op jit(solution)/shard_map/ppermute | solution.py:25
  21.2 15.4 %collective-permute-start = (f32[16,768]{1,0:T(8,128)}, f32[16,768]{1,0:T(8,128)}, u32[]{:S(2)}, u32[]{:S(2)}) collective-permute-start(f32[16,768]{1,0:T(8,128)} %get-tuple-element.99), channel_id=1, source_target_pairs={{0,1},{1,2},{2,3},{4,5},{5,6},{6,7},{8,9},{9,10},{10,11},{12,13},{... | collective-permute-start | bytes 147464 | tf_op jit(solution)/shard_map/ppermute | solution.py:22
  36.6 1.7 copy-start.8
  36.6 1.7 copy-start.25
  42.2 15.1 %collective-permute-start.3 = (f32[16,768]{1,0:T(8,128)}, f32[16,768]{1,0:T(8,128)}, u32[]{:S(2)}, u32[]{:S(2)}) collective-permute-start(f32[16,768]{1,0:T(8,128)} %get-tuple-element.98), channel_id=1, source_target_pairs={{1,0},{2,1},{3,2},{5,4},{6,5},{7,6},{9,8},{10,9},{11,10},{13,12},{... | collective-permute-start | bytes 147464 | tf_op jit(solution)/shard_map/ppermute | solution.py:25
  44.1 13.2 %collective-permute-start.2 = (f32[16,768]{1,0:T(8,128)}, f32[16,768]{1,0:T(8,128)}, u32[]{:S(2)}, u32[]{:S(2)}) collective-permute-start(f32[16,768]{1,0:T(8,128)} %get-tuple-element.97), channel_id=1, source_target_pairs={{0,1},{1,2},{2,3},{4,5},{5,6},{6,7},{8,9},{9,10},{10,11},{12,13},{... | collective-permute-start | bytes 147464 | tf_op jit(solution)/shard_map/ppermute | solution.py:22
  57.3 1.7 copy-start.7
  57.3 1.7 copy-start.19
  62.8 15.1 %collective-permute-start.5 = (f32[16,768]{1,0:T(8,128)}, f32[16,768]{1,0:T(8,128)}, u32[]{:S(2)}, u32[]{:S(2)}) collective-permute-start(f32[16,768]{1,0:T(8,128)} %get-tuple-element.96), channel_id=1, source_target_pairs={{1,0},{2,1},{3,2},{5,4},{6,5},{7,6},{9,8},{10,9},{11,10},{13,12},{... | collective-permute-start | bytes 147464 | tf_op jit(solution)/shard_map/ppermute | solution.py:25
  64.7 13.2 %collective-permute-start.4 = (f32[16,768]{1,0:T(8,128)}, f32[16,768]{1,0:T(8,128)}, u32[]{:S(2)}, u32[]{:S(2)}) collective-permute-start(f32[16,768]{1,0:T(8,128)} %get-tuple-element.95), channel_id=1, source_target_pairs={{0,1},{1,2},{2,3},{4,5},{5,6},{6,7},{8,9},{9,10},{10,11},{12,13},{... | collective-permute-start | bytes 147464 | tf_op jit(solution)/shard_map/ppermute | solution.py:22
  77.9 1.7 copy-start.5
  77.9 1.7 copy-start.13
  83.4 16.4 %collective-permute-start.7 = (f32[16,768]{1,0:T(8,128)}, f32[16,768]{1,0:T(8,128)}, u32[]{:S(2)}, u32[]{:S(2)}) collective-permute-start(f32[16,768]{1,0:T(8,128)} %get-tuple-element.94), channel_id=1, source_target_pairs={{1,0},{2,1},{3,2},{5,4},{6,5},{7,6},{9,8},{10,9},{11,10},{13,12},{... | collective-permute-start | bytes 147464 | tf_op jit(solution)/shard_map/ppermute | solution.py:25
  85.3 14.5 %collective-permute-start.6 = (f32[16,768]{1,0:T(8,128)}, f32[16,768]{1,0:T(8,128)}, u32[]{:S(2)}, u32[]{:S(2)}) collective-permute-start(f32[16,768]{1,0:T(8,128)} %get-tuple-element.93), channel_id=1, source_target_pairs={{0,1},{1,2},{2,3},{4,5},{5,6},{6,7},{8,9},{9,10},{10,11},{12,13},{... | collective-permute-start | bytes 147464 | tf_op jit(solution)/shard_map/ppermute | solution.py:22
  99.8 1.7 copy-start.3
  103.9 1.6 copy-start.9
  106.8 130.5 %all-gather.5.cloned.1.call-start = ((), (), s32[]{:S(2)}) async-start(), calls=%async_computation.1 | async-start | bytes 2949120 | tf_op jit(solution)/shard_map/all_gather | solution.py:69
  243.2 1.5 copy-start.1
  250.5 1.5 copy-start.1
  287.0 1.5 copy-start.1
  294.2 1.5 copy-start.1
  300.0 1.6 copy-start.10
  (26 other events, 29.4 us)
Sparse Core Ops, SparseCore 0:
  106.9 66.3 all-gather.2
  176.3 60.9 all-gather.4
where the time goes:
time: 340 us; the launch traced here: 337 us
  waiting for transfers between devices  124 us (36%)
  starting transfers between devices  54 us (16%)
  local copies, waits for them, and re-layouts  48 us (14%)
  matrix products  46.4 us (14%)
  between operations  27 us (8%)
  other arithmetic  25.6 us (8%)
  blocking collectives  12.2 us (4%)
    all_gather x1, waiting for transfers between devices, body(): piece_keys = lax.all_gather(key_rows, 'seq', axis=0, tiled=True)  63.7 us
    all_gather x1, waiting for transfers between devices, body(): piece_values = lax.all_gather(value_rows, 'seq', axis=0, tiled=True)  59.7 us
    ppermute x4, starting transfers between devices, with_halo(): lax.ppermute(lax.slice_in_dim(block, block.shape[dim] - width, None, axis...  35.6 us
    dot_general x8, matrix products, per_head(): jnp.dot(probs.astype(jnp.bfloat16), value_head, preferred_element_type=jn...  23.5 us
    ppermute x4, starting transfers between devices, with_halo(): lax.ppermute(lax.slice_in_dim(block, 0, width, axis=dim), axis, backward)  18.1 us
    dot_general x8, matrix products, per_head(): jnp.dot(query_head, key_head.T, preferred_element_type=jnp.float32)  12.6 us
    all_gather x1, blocking collectives, body(): piece = lax.all_gather(right_local, 'seq', axis=0, tiled=True)  12.2 us
    dynamic_update_slice x8, local copies, waits for them, and re-layouts, body(): lax.map(per_head, (initial[0], initial[1], initial[2], query_heads, key_h...  10.6 us
  transfers between devices with their start and end apart: 10, of which 2 were waited for; matrix products, arithmetic and copies ran while one was open for 4% of the time, Pallas kernels for 0%

commit v1 on v0

v1 whole, which is shorter than its diff:
```python
import math

import jax
import jax.numpy as jnp
from jax import lax
from jax.experimental import pallas as pl
from jax.experimental.pallas import tpu as pltpu
from jax.sharding import PartitionSpec as P

C = 768
HEADS = 8
KSIZE = 5
LAYERS = 4
POOL = 16
PCH = 64
R = 8
ROWS = 384
GROUP = 4
LANES = 128
CT = C // LANES
REACH = 16
EDGE = LAYERS * REACH
SEG = ROWS // 8
CHUNK = 128
PAIRS = HEADS // 2
WIN = 256
BF = jnp.bfloat16
F32 = jnp.float32
MESH = pl.DeviceIdType.MESH
LOG2E = math.log2(math.e)


def gelu(v):
    u = v * (math.sqrt(2 / math.pi) + math.sqrt(2 / math.pi) * 0.044715 * (v * v))
    half = 0.5 * v
    return half + half * jnp.tanh(u)


def conv_stack(nat, seg, hbuf, taps_ref, dil_ref, low, high):
    def load(q, _):
        for c in range(CT):
            seg[c, q] = nat[c, pl.ds(q, 8, stride=SEG), :]
        return 0

    lax.fori_loop(0, SEG, load, 0)

    def layer(l, _):
        d = dil_ref[l]

        def norm(k, _):
            q = pl.multiple_of(k * 8, 8)
            rows = [seg[c, pl.ds(q, 8)] for c in range(CT)]
            total = rows[0] * rows[0]
            for c in range(1, CT):
                total = total + rows[c] * rows[c]
            mean = jnp.sum(total, axis=-1, keepdims=True) * (1.0 / C)
            place = (
                lax.broadcasted_iota(jnp.int32, (8, 8, 1), 1) * SEG
                + lax.broadcasted_iota(jnp.int32, (8, 8, 1), 0)
                + q
            )
            scale = jnp.where((place >= low) & (place < high), lax.rsqrt(mean + 1e-06), 0.0)
            for c in range(CT):
                hbuf[c, pl.ds(q + REACH, 8)] = rows[c] * scale
            return 0

        lax.fori_loop(0, SEG // 8, norm, 0)
        for c in range(CT):
            hbuf[c, 0:REACH] = pltpu.roll(hbuf[c, SEG : SEG + REACH], 1, 1)
            hbuf[c, SEG + REACH : SEG + 2 * REACH] = pltpu.roll(
                hbuf[c, REACH : 2 * REACH], 7, 1
            )
        for c in range(CT):
            cols = slice(c * LANES, (c + 1) * LANES)
            taps = [
                jnp.broadcast_to(taps_ref[l, t : t + 1, cols], (8, LANES))[None]
                for t in range(KSIZE)
            ]

            def conv(k, _):
                q = pl.multiple_of(k * 8, 8)
                total = taps[0] * hbuf[c, pl.ds(q + REACH - 2 * d, 8)]
                for t in range(1, KSIZE):
                    total = total + taps[t] * hbuf[c, pl.ds(q + REACH + (t - 2) * d, 8)]
                seg[c, pl.ds(q, 8)] = seg[c, pl.ds(q, 8)] + gelu(total)
                return 0

            lax.fori_loop(0, SEG // 8, conv, 0)
        return 0

    lax.fori_loop(0, LAYERS, layer, 0)

    def store(q, _):
        for c in range(CT):
            nat[c, pl.ds(q, 8, stride=SEG), :] = seg[c, q]
        return 0

    lax.fori_loop(0, SEG, store, 0)


def kernel(
    x_ref, gain_ref, taps_ref, dil_ref, again_ref, wqkv_hbm, wout_hbm, wa_hbm, wb_hbm,
    track_ref, pair_ref,
    wqkv, wout, wa, wb, scaled, nat, seg, hbuf, state, halo, near, far, keys, values, q2,
    top, mass, acc, mixed, rights, wsem, send, recv,
):
    block = lax.axis_index("seq")
    core = lax.rem(block, 2)
    sibling = block + 1 - 2 * core
    partner = lax.rem(block + 2, GROUP)
    cross = GROUP - 1 - block

    def remote(src, dst, index, target):
        return pltpu.make_async_remote_copy(
            src_ref=src, dst_ref=dst, send_sem=send.at[index], recv_sem=recv.at[index],
            device_id={"seq": target}, device_id_type=MESH,
        )

    weights = [
        pltpu.make_async_copy(src, dst, wsem.at[i])
        for i, (src, dst) in enumerate(
            ((wqkv_hbm, wqkv), (wout_hbm, wout), (wa_hbm, wa), (wb_hbm, wb))
        )
    ]
    for copy in weights:
        copy.start()
    barrier = pltpu.get_barrier_semaphore()
    for target in (sibling, partner, cross):
        pl.semaphore_signal(barrier, inc=1, device_id={"seq": target}, device_id_type=MESH)

    for l in range(LAYERS):
        scaled[l] = taps_ref[l] * gain_ref[l : l + 1]
    for c in range(CT):
        nat[c] = x_ref[:, c * LANES : (c + 1) * LANES].astype(F32)
    conv_stack(nat, seg, hbuf, scaled, dil_ref, 0, ROWS)

    def finish(source, target, count):
        rows = [nat[c, source : source + count] for c in range(CT)]
        total = rows[0] * rows[0]
        for c in range(1, CT):
            total = total + rows[c] * rows[c]
        scale = lax.rsqrt(jnp.sum(total, axis=-1, keepdims=True) * (1.0 / C) + 1e-06)
        for c in range(CT):
            cols = slice(c * LANES, (c + 1) * LANES)
            state[c, target : target + count] = rows[c]
            near[0, target : target + count, cols] = (
                rows[c] * scale * again_ref[:, cols]
            ).astype(BF)

    for start in range(EDGE, ROWS - EDGE, 64):
        finish(start, start, 64)
    pl.semaphore_wait(barrier, 3)

    to_left = remote(x_ref.at[pl.ds(0, EDGE)], halo.at[1], 0, lax.rem(block + GROUP - 1, GROUP))
    to_right = remote(
        x_ref.at[pl.ds(ROWS - EDGE, EDGE)], halo.at[0], 1, lax.rem(block + 1, GROUP)
    )
    has_left, has_right = block > 0, block < GROUP - 1

    @pl.when(has_left)
    def _():
        to_left.start()

    @pl.when(has_right)
    def _():
        to_right.start()

    inner = [
        remote(near.at[0, pl.ds(EDGE + i * CHUNK, CHUNK)], far.at[2 * i], 2 + i, partner)
        for i in range(2)
    ]
    inner_near = remote(
        near.at[0, pl.ds(EDGE, 2 * CHUNK)], near.at[1, pl.ds(EDGE, 2 * CHUNK)], 6, sibling
    )
    inner_near.start()
    for copy in inner:
        copy.start()

    @pl.when(has_left)
    def _():
        to_right.wait_recv()

    @pl.when(jnp.logical_not(has_left))
    def _():
        halo[0] = jnp.zeros((EDGE, C), BF)

    @pl.when(has_right)
    def _():
        to_left.wait_recv()

    @pl.when(jnp.logical_not(has_right))
    def _():
        halo[1] = jnp.zeros((EDGE, C), BF)

    for c in range(CT):
        cols = slice(c * LANES, (c + 1) * LANES)
        nat[c, 0:EDGE] = halo[0, :, cols].astype(F32)
        nat[c, EDGE : 3 * EDGE] = x_ref[0 : 2 * EDGE, cols].astype(F32)
        nat[c, 3 * EDGE : 5 * EDGE] = x_ref[ROWS - 2 * EDGE :, cols].astype(F32)
        nat[c, 5 * EDGE :] = halo[1, :, cols].astype(F32)
    conv_stack(
        nat, seg, hbuf, scaled, dil_ref,
        jnp.where(has_left, 0, EDGE), jnp.where(has_right, ROWS, ROWS - EDGE),
    )
    finish(EDGE, 0, EDGE)
    finish(ROWS - 2 * EDGE, ROWS - EDGE, EDGE)
    outer = []
    for i, start in enumerate((0, ROWS - EDGE)):
        rows = pl.ds(start, EDGE)
        outer.append(remote(near.at[0, rows], far.at[4, pl.ds(i * EDGE, EDGE)], 4 + i, partner))
        outer.append(remote(near.at[0, rows], near.at[1, rows], 7 + i, sibling))
    for copy in outer:
        copy.start()

    weights[0].wait()

    lane = lax.broadcasted_iota(jnp.int32, (1, WIN), 1)

    def project(source, column):
        return jnp.dot(
            source, wqkv[:, pl.ds(pl.multiple_of(column, LANES), WIN)],
            preferred_element_type=F32,
        ).astype(BF)

    def window(p):
        return (p // 2) * (3 * LANES) + lax.rem(p, 2) * LANES

    def queries(p, _):
        rows = project(near[0], window(p))
        first = lax.rem(p, 2) * 64
        for i in range(2):
            mine = (lane >= first + 96 * i) & (lane < first + 96 * (i + 1))
            q2[p, i * ROWS : (i + 1) * ROWS] = jnp.where(mine, rows, jnp.zeros_like(rows))
        return 0

    lax.fori_loop(0, PAIRS, queries, 0)

    def keys_values(load, place, count):
        def tile(t, _):
            cols = pl.ds(pl.multiple_of(t * WIN, WIN), WIN)
            source = load()
            keys[place : place + count, cols] = project(source, C + t * WIN)
            values[place : place + count, cols] = project(source, 2 * C + t * WIN)
            return 0

        lax.fori_loop(0, C // WIN, tile, 0)

    TILE = 256
    SCALE = LOG2E / math.sqrt(C // HEADS)

    def attend(place, count, fresh):
        def pair(p, _):
            cols = pl.ds(pl.multiple_of(window(p), LANES), WIN)

            def tile(t, _):
                rows = pl.ds(pl.multiple_of(t * TILE, TILE), TILE)
                scores = lax.dot_general(
                    q2[p, rows], keys[place : place + count, cols],
                    (((1,), (1,)), ((), ())), preferred_element_type=F32,
                )
                peak = jnp.max(scores, axis=-1, keepdims=True)
                if not fresh:
                    old = top[p, rows]
                    peak = jnp.maximum(peak, old)
                probs = jnp.exp2((scores - peak) * SCALE)
                part = jnp.sum(probs, axis=-1, keepdims=True)
                out = jnp.dot(
                    probs.astype(BF), values[place : place + count, cols],
                    preferred_element_type=F32,
                )
                if fresh:
                    mass[p, rows] = part
                    acc[p, rows] = out
                else:
                    rescale = jnp.exp2((old - peak) * SCALE)
                    mass[p, rows] = mass[p, rows] * rescale + part
                    acc[p, rows] = acc[p, rows] * rescale + out
                top[p, rows] = peak
                return 0

            lax.fori_loop(0, 2 * ROWS // TILE, tile, 0)
            return 0

        lax.fori_loop(0, PAIRS, pair, 0)

    keys_values(lambda: near[0], 0, ROWS)
    inner_near.wait_recv()
    outer[1].wait_recv()
    outer[3].wait_recv()
    keys_values(lambda: near[1], ROWS, ROWS)
    attend(0, 2 * ROWS, True)

    passes = []
    for i in range(3):
        for copy in ([inner[i]] if i < 2 else [outer[0], outer[2]]):
            copy.wait_recv()
        onward = remote(far.at[2 * i], far.at[2 * i + 1], 9 + i, sibling)
        onward.start()
        passes.append(onward)
        onward.wait_recv()
        place = 2 * ROWS + 2 * CHUNK * i
        keys_values(
            lambda i=i: far[2 * i : 2 * i + 2].reshape(2 * CHUNK, C), place, 2 * CHUNK
        )
        attend(place, 2 * CHUNK, False)

    for g in range(2):
        parts = []
        for j in range(2):
            p = 2 * g + j
            both = acc[p] / mass[p]
            first = j * 64
            one = (lane >= first) & (lane < first + 96)
            two = (lane >= first + 96) & (lane < first + 192)
            parts.append(
                jnp.where(one, both[:ROWS], jnp.where(two, both[ROWS:], 0.0))
            )
        base = g * 3 * LANES
        mixed[:, base : base + LANES] = parts[0][:, :LANES].astype(BF)
        mixed[:, base + LANES : base + 2 * LANES] = (
            parts[0][:, LANES:] + parts[1][:, :LANES]
        ).astype(BF)
        mixed[:, base + 2 * LANES : base + 3 * LANES] = parts[1][:, LANES:].astype(BF)

    weights[1].wait()
    squares = jnp.zeros((ROWS // POOL, LANES), F32)
    pools = []
    for t in range(C // WIN):
        product = jnp.dot(
            mixed[...], wout[:, t * WIN : (t + 1) * WIN], preferred_element_type=F32
        )
        for j in range(WIN // LANES):
            c = t * (WIN // LANES) + j
            result = state[c] + product[:, j * LANES : (j + 1) * LANES]
            track_ref[:, c * LANES : (c + 1) * LANES] = result.astype(BF)
            pool = jnp.sum(result.reshape(ROWS // POOL, POOL, LANES), axis=1) * (1.0 / POOL)
            squares = squares + pool * pool
            pools.append(pool)
    scale = lax.rsqrt(jnp.sum(squares, axis=-1, keepdims=True) * (1.0 / C) + 1e-06)
    pooled = jnp.concatenate([pool * scale for pool in pools], axis=1).astype(BF)
    weights[3].wait()
    right = jnp.dot(pooled, wb[...], preferred_element_type=F32).astype(BF)
    rights[pl.ds(block, 1)] = right[None]
    shares = [
        remote(rights.at[block], rights.at[block], 12 + i, target)
        for i, target in enumerate((sibling, partner, cross))
    ]
    for copy in shares[::-1]:
        copy.start()
    weights[2].wait()
    left = jnp.dot(pooled, wa[...], preferred_element_type=F32).astype(BF).astype(F32)
    channel = lax.rem(lax.broadcasted_iota(jnp.int32, (PCH, 1, R * PCH), 2), PCH)
    wanted = lax.broadcasted_iota(jnp.int32, (PCH, 1, R * PCH), 0)
    spread = jnp.where(channel == wanted, left[None], 0.0)
    spread = spread.reshape(PCH * (ROWS // POOL), R * PCH).astype(BF)
    for copy in shares:
        copy.wait_recv()
    every = jnp.concatenate([rights[i].astype(F32) for i in range(GROUP)], axis=0).astype(BF)
    product = lax.dot_general(
        spread, every, (((1,), (1,)), ((), ())), preferred_element_type=F32
    )
    pair_ref[...] = (
        (product * (1.0 / math.sqrt(R))).reshape(PCH, ROWS // POOL, GROUP * ROWS // POOL)
    ).astype(BF)

    @pl.when(has_left)
    def _():
        to_left.wait_send()

    @pl.when(has_right)
    def _():
        to_right.wait_send()

    for copy in inner + [inner_near] + outer + passes + shares:
        copy.wait_send()


def body(x, conv_gain, conv_kernel, dilation, attn_gain, w_qkv, w_out, w_pair_a, w_pair_b):
    vmem = pl.BlockSpec(memory_space=pltpu.VMEM)
    hbm = pl.BlockSpec(memory_space=pl.ANY)
    return pl.pallas_call(
        kernel,
        out_shape=(
            jax.ShapeDtypeStruct((ROWS, C), BF),
            jax.ShapeDtypeStruct((PCH, ROWS // POOL, GROUP * ROWS // POOL), BF),
        ),
        in_specs=[vmem, vmem, vmem, pl.BlockSpec(memory_space=pltpu.SMEM), vmem, hbm, hbm, hbm, hbm],
        out_specs=(vmem, vmem),
        scratch_shapes=[
            pltpu.VMEM(w_qkv.shape, BF),
            pltpu.VMEM(w_out.shape, BF),
            pltpu.VMEM(w_pair_a.shape, BF),
            pltpu.VMEM(w_pair_b.shape, BF),
            pltpu.VMEM((LAYERS, KSIZE, C), F32),
            pltpu.VMEM((CT, ROWS, LANES), F32),
            pltpu.VMEM((CT, SEG, 8, LANES), F32),
            pltpu.VMEM((CT, SEG + 2 * REACH, 8, LANES), F32),
            pltpu.VMEM((CT, ROWS, LANES), F32),
            pltpu.VMEM((2, EDGE, C), BF),
            pltpu.VMEM((2, ROWS, C), BF),
            pltpu.VMEM((6, CHUNK, C), BF),
            pltpu.VMEM((GROUP * ROWS, C), BF),
            pltpu.VMEM((GROUP * ROWS, C), BF),
            pltpu.VMEM((PAIRS, 2 * ROWS, WIN), BF),
            pltpu.VMEM((PAIRS, 2 * ROWS, 1), F32),
            pltpu.VMEM((PAIRS, 2 * ROWS, 1), F32),
            pltpu.VMEM((PAIRS, 2 * ROWS, WIN), F32),
            pltpu.VMEM((ROWS, C), BF),
            pltpu.VMEM((GROUP, ROWS // POOL, R * PCH), BF),
            pltpu.SemaphoreType.DMA((4,)),
            pltpu.SemaphoreType.DMA((15,)),
            pltpu.SemaphoreType.DMA((15,)),
        ],
        compiler_params=pltpu.CompilerParams(
            collective_id=0, has_side_effects=True, vmem_limit_bytes=60 * 1024 * 1024
        ),
    )(x, conv_gain, conv_kernel, dilation, attn_gain.reshape(1, C), w_qkv, w_out, w_pair_a, w_pair_b)


def solution(mesh):
    placed = (P(("batch", "seq"), None), P(), P(), P(), P(), P(), P(), P(), P())
    return jax.shard_map(
        body,
        mesh=mesh,
        in_specs=placed,
        out_specs=(P(("batch", "seq"), None), P("batch", "seq", None)),
        check_vma=False,
    )
```

time: 340 us -> 111 us (0.33)
  the two profiles are of different devices: /device:TPU:1 before, /device:TPU:257 now
where the time goes in v1:
time: 111 us
  Pallas kernels  104 us (94%)
  local copies, waits for them, and re-layouts  6.45 us (6%)
    pallas_call x1, Pallas kernels, body(): pl.pallas_call(kernel, out_shape=(jax.ShapeDtypeStruct((ROWS, C), BF), ja...  104 us
    unnamed x3, local copies, waits for them, and re-layouts  5.19 us

profile of v1, /device:TPU:257, one launch (start us, length us, event | category | flops | bytes accessed | tf_op | source)
XLA Modules:
  0.0 110.6 jit_solution(15002531015792449113)
XLA Ops:
  0.6 1.3 %reshape.7.again_ref = f32[1,768]{1,0:T(1,128)} reshape(f32[768]{0:T(1024)} %param.13) | data formatting | bytes 6144 | tf_op jit(solution)/shard_map/reshape | solution.py:417
  1.9 1.5 %copy.11.taps_ref = f32[4,5,768]{2,1,0:T(8,128)} copy(f32[4,5,768]{2,0,1:T(4,128)} %param.11) | data formatting | bytes 122880 | tf_op args[2]
  3.4 103.5 %shard_map.104 = (bf16[384,768]{1,0:T(8,128)(2,1)}, bf16[64,24,96]{2,1,0:T(8,128)(2,1)}) custom-call(bf16[384,768]{1,0:T(8,128)(2,1)} %x_ref.1, f32[4,768]{1,0:T(4,128)} %gain_ref.1, f32[4,5,768]{2,1,0:T(8,128)} %copy.11.taps_ref, s32[4]{0:T(128)} %dil_ref.1, f32[1,768]{1,0:T(1,128)} %reshape.7.again_ref, bf16[768,2304]{1,0:T(8,128)(2,1)} %wqkv_hbm.1, ...), custom_call_target="tpu_custom_call" | custom-call | tf_op jit(solution)/shard_map/pallas_call | solution.py:381
  106.9 1.9 %copy.14 = bf16[384,768]{1,0:T(8,128)(2,1)} copy(bf16[384,768]{1,0:T(8,128)(2,1)} %get-tuple-element.4) | data formatting | bytes 1179648
  108.9 1.8 %copy.15 = bf16[64,24,96]{2,1,0:T(8,128)(2,1)} copy(bf16[64,24,96]{2,1,0:T(8,128)(2,1)} %get-tuple-element.5) | data formatting | bytes 589824

commit v2 on v1

--- a/solution.py
+++ b/solution.py
@@ -21,6 +21,7 @@
 REACH = 16
 EDGE = LAYERS * REACH
 SEG = ROWS // 8
+STEP = 8
 CHUNK = 128
 PAIRS = HEADS // 2
 WIN = 256
@@ -37,19 +38,20 @@
 
 
 def conv_stack(nat, seg, hbuf, taps_ref, dil_ref, low, high):
-    def load(q, _):
-        for c in range(CT):
-            seg[c, q] = nat[c, pl.ds(q, 8, stride=SEG), :]
+    def load(k, _):
+        for j in range(8):
+            q = k * 8 + j
+            for c in range(CT):
+                seg[c, q] = nat[c, pl.ds(q, 8, stride=SEG), :]
         return 0
 
-    lax.fori_loop(0, SEG, load, 0)
+    lax.fori_loop(0, SEG // 8, load, 0)
 
     def layer(l, _):
         d = dil_ref[l]
 
-        def norm(k, _):
-            q = pl.multiple_of(k * 8, 8)
-            rows = [seg[c, pl.ds(q, 8)] for c in range(CT)]
+        for q in range(0, SEG, 8):
+            rows = [seg[c, q : q + 8] for c in range(CT)]
             total = rows[0] * rows[0]
             for c in range(1, CT):
                 total = total + rows[c] * rows[c]
@@ -61,10 +63,7 @@
             )
             scale = jnp.where((place >= low) & (place < high), lax.rsqrt(mean + 1e-06), 0.0)
             for c in range(CT):
-                hbuf[c, pl.ds(q + REACH, 8)] = rows[c] * scale
-            return 0
-
-        lax.fori_loop(0, SEG // 8, norm, 0)
+                hbuf[c, q + REACH : q + REACH + 8] = rows[c] * scale
         for c in range(CT):
             hbuf[c, 0:REACH] = pltpu.roll(hbuf[c, SEG : SEG + REACH], 1, 1)
             hbuf[c, SEG + REACH : SEG + 2 * REACH] = pltpu.roll(
@@ -77,32 +76,30 @@
                 for t in range(KSIZE)
             ]
 
-            def conv(k, _):
-                q = pl.multiple_of(k * 8, 8)
-                total = taps[0] * hbuf[c, pl.ds(q + REACH - 2 * d, 8)]
+            for q in range(0, SEG, STEP):
+                total = taps[0] * hbuf[c, pl.ds(q + REACH - 2 * d, STEP)]
                 for t in range(1, KSIZE):
-                    total = total + taps[t] * hbuf[c, pl.ds(q + REACH + (t - 2) * d, 8)]
-                seg[c, pl.ds(q, 8)] = seg[c, pl.ds(q, 8)] + gelu(total)
-                return 0
-
-            lax.fori_loop(0, SEG // 8, conv, 0)
+                    total = total + taps[t] * hbuf[c, pl.ds(q + REACH + (t - 2) * d, STEP)]
+                seg[c, q : q + STEP] = seg[c, q : q + STEP] + gelu(total)
         return 0
 
     lax.fori_loop(0, LAYERS, layer, 0)
 
-    def store(q, _):
-        for c in range(CT):
-            nat[c, pl.ds(q, 8, stride=SEG), :] = seg[c, q]
+    def store(k, _):
+        for j in range(8):
+            q = k * 8 + j
+            for c in range(CT):
+                nat[c, pl.ds(q, 8, stride=SEG), :] = seg[c, q]
         return 0
 
-    lax.fori_loop(0, SEG, store, 0)
+    lax.fori_loop(0, SEG // 8, store, 0)
 
 
 def kernel(
     x_ref, gain_ref, taps_ref, dil_ref, again_ref, wqkv_hbm, wout_hbm, wa_hbm, wb_hbm,
-    track_ref, pair_ref,
+    track_ref, left_ref, rights,
     wqkv, wout, wa, wb, scaled, nat, seg, hbuf, state, halo, near, far, keys, values, q2,
-    top, mass, acc, mixed, rights, wsem, send, recv,
+    top, acc, mixed, wsem, send, recv,
 ):
     block = lax.axis_index("seq")
     core = lax.rem(block, 2)
@@ -128,8 +125,10 @@
     for target in (sibling, partner, cross):
         pl.semaphore_signal(barrier, inc=1, device_id={"seq": target}, device_id_type=MESH)
 
-    for l in range(LAYERS):
-        scaled[l] = taps_ref[l] * gain_ref[l : l + 1]
+    for t in range(KSIZE):
+        product = taps_ref[t] * gain_ref[...]
+        for l in range(LAYERS):
+            scaled[l, t : t + 1] = product[l : l + 1]
     for c in range(CT):
         nat[c] = x_ref[:, c * LANES : (c + 1) * LANES].astype(F32)
     conv_stack(nat, seg, hbuf, scaled, dil_ref, 0, ROWS)
@@ -144,7 +143,7 @@
             cols = slice(c * LANES, (c + 1) * LANES)
             state[c, target : target + count] = rows[c]
             near[0, target : target + count, cols] = (
-                rows[c] * scale * again_ref[:, cols]
+                rows[c] * scale * again_ref[cols][None]
             ).astype(BF)
 
     for start in range(EDGE, ROWS - EDGE, 64):
@@ -173,8 +172,7 @@
         near.at[0, pl.ds(EDGE, 2 * CHUNK)], near.at[1, pl.ds(EDGE, 2 * CHUNK)], 6, sibling
     )
     inner_near.start()
-    for copy in inner:
-        copy.start()
+    inner[0].start()
 
     @pl.when(has_left)
     def _():
@@ -209,8 +207,8 @@
         rows = pl.ds(start, EDGE)
         outer.append(remote(near.at[0, rows], far.at[4, pl.ds(i * EDGE, EDGE)], 4 + i, partner))
         outer.append(remote(near.at[0, rows], near.at[1, rows], 7 + i, sibling))
-    for copy in outer:
-        copy.start()
+    outer[1].start()
+    outer[3].start()
 
     weights[0].wait()
 
@@ -218,78 +216,74 @@
 
     def project(source, column):
         return jnp.dot(
-            source, wqkv[:, pl.ds(pl.multiple_of(column, LANES), WIN)],
-            preferred_element_type=F32,
+            source, wqkv[:, column : column + WIN], preferred_element_type=F32
         ).astype(BF)
 
     def window(p):
-        return (p // 2) * (3 * LANES) + lax.rem(p, 2) * LANES
-
-    def queries(p, _):
+        return (p // 2) * (3 * LANES) + (p % 2) * LANES
+
+    for p in range(PAIRS):
         rows = project(near[0], window(p))
-        first = lax.rem(p, 2) * 64
+        first = (p % 2) * 64
         for i in range(2):
             mine = (lane >= first + 96 * i) & (lane < first + 96 * (i + 1))
             q2[p, i * ROWS : (i + 1) * ROWS] = jnp.where(mine, rows, jnp.zeros_like(rows))
-        return 0
-
-    lax.fori_loop(0, PAIRS, queries, 0)
-
-    def keys_values(load, place, count):
-        def tile(t, _):
-            cols = pl.ds(pl.multiple_of(t * WIN, WIN), WIN)
-            source = load()
-            keys[place : place + count, cols] = project(source, C + t * WIN)
-            values[place : place + count, cols] = project(source, 2 * C + t * WIN)
-            return 0
-
-        lax.fori_loop(0, C // WIN, tile, 0)
+
+    def spare(p):
+        first = (p % 2) * 64
+        return (lane < first) | (lane >= first + 192)
+
+    def keys_values(source, place, count):
+        for t in range(C // WIN):
+            keys[place : place + count, t * WIN : (t + 1) * WIN] = project(source, C + t * WIN)
+        for p in range(PAIRS):
+            rows = project(source, 2 * C + window(p))
+            values[p, place : place + count] = jnp.where(spare(p), jnp.ones_like(rows), rows)
 
     TILE = 256
     SCALE = LOG2E / math.sqrt(C // HEADS)
 
     def attend(place, count, fresh):
-        def pair(p, _):
-            cols = pl.ds(pl.multiple_of(window(p), LANES), WIN)
-
-            def tile(t, _):
-                rows = pl.ds(pl.multiple_of(t * TILE, TILE), TILE)
+        for p in range(PAIRS):
+            cols = slice(window(p), window(p) + WIN)
+            for t in range(2 * ROWS // TILE):
+                rows = slice(t * TILE, (t + 1) * TILE)
                 scores = lax.dot_general(
                     q2[p, rows], keys[place : place + count, cols],
                     (((1,), (1,)), ((), ())), preferred_element_type=F32,
                 )
-                peak = jnp.max(scores, axis=-1, keepdims=True)
+                pieces = [scores[:, j : j + LANES] for j in range(0, count, LANES)]
+                peak = pieces[0]
+                for piece in pieces[1:]:
+                    peak = jnp.maximum(peak, piece)
+                peak = jnp.broadcast_to(jnp.max(peak, axis=-1, keepdims=True), (TILE, LANES))
                 if not fresh:
                     old = top[p, rows]
                     peak = jnp.maximum(peak, old)
-                probs = jnp.exp2((scores - peak) * SCALE)
-                part = jnp.sum(probs, axis=-1, keepdims=True)
+                top[p, rows] = peak
+                probs = jnp.concatenate(
+                    [jnp.exp2((piece - peak) * SCALE).astype(BF) for piece in pieces], axis=1
+                )
                 out = jnp.dot(
-                    probs.astype(BF), values[place : place + count, cols],
-                    preferred_element_type=F32,
+                    probs, values[p, place : place + count], preferred_element_type=F32
                 )
                 if fresh:
-                    mass[p, rows] = part
                     acc[p, rows] = out
                 else:
                     rescale = jnp.exp2((old - peak) * SCALE)
-                    mass[p, rows] = mass[p, rows] * rescale + part
-                    acc[p, rows] = acc[p, rows] * rescale + out
-                top[p, rows] = peak
-                return 0
-
-            lax.fori_loop(0, 2 * ROWS // TILE, tile, 0)
-            return 0
-
-        lax.fori_loop(0, PAIRS, pair, 0)
-
-    keys_values(lambda: near[0], 0, ROWS)
+                    for j in range(0, WIN, LANES):
+                        acc[p, rows, j : j + LANES] = (
+                            acc[p, rows, j : j + LANES] * rescale + out[:, j : j + LANES]
+                        )
+
     inner_near.wait_recv()
     outer[1].wait_recv()
     outer[3].wait_recv()
-    keys_values(lambda: near[1], ROWS, ROWS)
+    keys_values(near[...].reshape(2 * ROWS, C), 0, 2 * ROWS)
     attend(0, 2 * ROWS, True)
 
+    inner[0].wait_send()
+    inner[1].start()
     passes = []
     for i in range(3):
         for copy in ([inner[i]] if i < 2 else [outer[0], outer[2]]):
@@ -297,18 +291,20 @@
         onward = remote(far.at[2 * i], far.at[2 * i + 1], 9 + i, sibling)
         onward.start()
         passes.append(onward)
+        if i == 0:
+            inner[1].wait_send()
+            outer[0].start()
+            outer[2].start()
         onward.wait_recv()
         place = 2 * ROWS + 2 * CHUNK * i
-        keys_values(
-            lambda i=i: far[2 * i : 2 * i + 2].reshape(2 * CHUNK, C), place, 2 * CHUNK
-        )
+        keys_values(far[2 * i : 2 * i + 2].reshape(2 * CHUNK, C), place, 2 * CHUNK)
         attend(place, 2 * CHUNK, False)
 
     for g in range(2):
         parts = []
         for j in range(2):
             p = 2 * g + j
-            both = acc[p] / mass[p]
+            both = acc[p] / acc[p, :, 192 * (1 - j) : 192 * (1 - j) + 1]
             first = j * 64
             one = (lane >= first) & (lane < first + 96)
             two = (lane >= first + 96) & (lane < first + 192)
@@ -348,44 +344,51 @@
     for copy in shares[::-1]:
         copy.start()
     weights[2].wait()
-    left = jnp.dot(pooled, wa[...], preferred_element_type=F32).astype(BF).astype(F32)
+    left_ref[...] = jnp.dot(pooled, wa[...], preferred_element_type=F32).astype(BF)
+    for copy in shares:
+        copy.wait_recv()
+    @pl.when(has_left)
+    def _():
+        to_left.wait_send()
+
+    @pl.when(has_right)
+    def _():
+        to_right.wait_send()
+
+    for copy in [inner_near] + outer + passes + shares:
+        copy.wait_send()
+
+
+def finale(track_hbm, left_ref, rights_ref, track_out, pair_ref, sem):
+    copy = pltpu.make_async_copy(track_hbm, track_out, sem)
+    copy.start()
+    left = left_ref[...].astype(F32)
     channel = lax.rem(lax.broadcasted_iota(jnp.int32, (PCH, 1, R * PCH), 2), PCH)
     wanted = lax.broadcasted_iota(jnp.int32, (PCH, 1, R * PCH), 0)
     spread = jnp.where(channel == wanted, left[None], 0.0)
     spread = spread.reshape(PCH * (ROWS // POOL), R * PCH).astype(BF)
-    for copy in shares:
-        copy.wait_recv()
-    every = jnp.concatenate([rights[i].astype(F32) for i in range(GROUP)], axis=0).astype(BF)
+    every = jnp.concatenate([rights_ref[i].astype(F32) for i in range(GROUP)], axis=0).astype(BF)
     product = lax.dot_general(
         spread, every, (((1,), (1,)), ((), ())), preferred_element_type=F32
     )
     pair_ref[...] = (
         (product * (1.0 / math.sqrt(R))).reshape(PCH, ROWS // POOL, GROUP * ROWS // POOL)
     ).astype(BF)
-
-    @pl.when(has_left)
-    def _():
-        to_left.wait_send()
-
-    @pl.when(has_right)
-    def _():
-        to_right.wait_send()
-
-    for copy in inner + [inner_near] + outer + passes + shares:
-        copy.wait_send()
+    copy.wait()
 
 
 def body(x, conv_gain, conv_kernel, dilation, attn_gain, w_qkv, w_out, w_pair_a, w_pair_b):
     vmem = pl.BlockSpec(memory_space=pltpu.VMEM)
     hbm = pl.BlockSpec(memory_space=pl.ANY)
-    return pl.pallas_call(
+    track, left, rights = pl.pallas_call(
         kernel,
         out_shape=(
             jax.ShapeDtypeStruct((ROWS, C), BF),
-            jax.ShapeDtypeStruct((PCH, ROWS // POOL, GROUP * ROWS // POOL), BF),
+            jax.ShapeDtypeStruct((ROWS // POOL, R * PCH), BF),
+            jax.ShapeDtypeStruct((GROUP, ROWS // POOL, R * PCH), BF),
         ),
         in_specs=[vmem, vmem, vmem, pl.BlockSpec(memory_space=pltpu.SMEM), vmem, hbm, hbm, hbm, hbm],
-        out_specs=(vmem, vmem),
+        out_specs=(vmem, vmem, vmem),
         scratch_shapes=[
             pltpu.VMEM(w_qkv.shape, BF),
             pltpu.VMEM(w_out.shape, BF),
@@ -400,13 +403,11 @@
             pltpu.VMEM((2, ROWS, C), BF),
             pltpu.VMEM((6, CHUNK, C), BF),
             pltpu.VMEM((GROUP * ROWS, C), BF),
-            pltpu.VMEM((GROUP * ROWS, C), BF),
+            pltpu.VMEM((PAIRS, GROUP * ROWS, WIN), BF),
             pltpu.VMEM((PAIRS, 2 * ROWS, WIN), BF),
-            pltpu.VMEM((PAIRS, 2 * ROWS, 1), F32),
-            pltpu.VMEM((PAIRS, 2 * ROWS, 1), F32),
+            pltpu.VMEM((PAIRS, 2 * ROWS, LANES), F32),
             pltpu.VMEM((PAIRS, 2 * ROWS, WIN), F32),
             pltpu.VMEM((ROWS, C), BF),
-            pltpu.VMEM((GROUP, ROWS // POOL, R * PCH), BF),
             pltpu.SemaphoreType.DMA((4,)),
             pltpu.SemaphoreType.DMA((15,)),
             pltpu.SemaphoreType.DMA((15,)),
@@ -414,7 +415,17 @@
         compiler_params=pltpu.CompilerParams(
             collective_id=0, has_side_effects=True, vmem_limit_bytes=60 * 1024 * 1024
         ),
-    )(x, conv_gain, conv_kernel, dilation, attn_gain.reshape(1, C), w_qkv, w_out, w_pair_a, w_pair_b)
+    )(x, conv_gain, conv_kernel.transpose(1, 0, 2), dilation, attn_gain, w_qkv, w_out, w_pair_a, w_pair_b)
+    return pl.pallas_call(
+        finale,
+        out_shape=(
+            jax.ShapeDtypeStruct((ROWS, C), BF),
+            jax.ShapeDtypeStruct((PCH, ROWS // POOL, GROUP * ROWS // POOL), BF),
+        ),
+        in_specs=[hbm, vmem, vmem],
+        out_specs=(hbm, vmem),
+        scratch_shapes=[pltpu.SemaphoreType.DMA],
+    )(track, left, rights)
 
 
 def solution(mesh):

time: 111 us -> 99.6 us (0.90)
  the two profiles are of different devices: /device:TPU:257 before, /device:TPU:311 now
where the time goes in v2:
time: 99.6 us; the launch traced here: 99.4 us
  Pallas kernels  98.6 us (99%)
    pallas_call x1, Pallas kernels, body(): pl.pallas_call(kernel, out_shape=(jax.ShapeDtypeStruct((ROWS, C), BF), ja...  77.9 us
    pallas_call x1, Pallas kernels, body(): pl.pallas_call(finale, out_shape=(jax.ShapeDtypeStruct((ROWS, C), BF), ja...  20.6 us

profile of v2, /device:TPU:311, one launch (start us, length us, event | category | flops | bytes accessed | tf_op | source)
XLA Modules:
  0.0 99.4 jit_solution(2840185188669544526)
XLA Ops:
  0.6 77.9 %shard_map.104 = (bf16[384,768]{1,0:T(8,128)(2,1)}, bf16[24,512]{1,0:T(8,128)(2,1)}, bf16[4,24,512]{2,1,0:T(8,128)(2,1)}) custom-call(bf16[384,768]{1,0:T(8,128)(2,1)} %x_ref.1, f32[4,768]{1,0:T(4,128)} %gain_ref.1, f32[5,4,768]{2,1,0:T(4,128)} %bitcast.1, s32[4]{0:T(128)} %dil_ref.1, f32[768]{0:T(1024)} %again_ref.1, bf16[768,2304]{1,0:T(8,128)(2,1)} %wqkv_hbm.1, ...), custom_call_target="tpu_custom_call" | custom-call | tf_op jit(solution)/shard_map/pallas_call | solution.py:383
  78.6 20.6 %shard_map.105 = (bf16[384,768]{1,0:T(8,128)(2,1)}, bf16[64,24,96]{2,1,0:T(8,128)(2,1)}) custom-call(bf16[384,768]{1,0:T(8,128)(2,1)} %get-tuple-element.5.track_hbm, bf16[24,512]{1,0:T(8,128)(2,1)} %get-tuple-element.6.left_ref, bf16[4,24,512]{2,1,0:T(8,128)(2,1)} %get-tuple-element.7.rights_ref), custom_call_target="tpu_custom_call" | custom-call | tf_op jit(solution)/shard_map/pallas_call | solution.py:419

commit v3 on v2

--- a/solution.py
+++ b/solution.py
@@ -173,6 +173,7 @@
     )
     inner_near.start()
     inner[0].start()
+    inner[1].start()
 
     @pl.when(has_left)
     def _():
@@ -283,7 +284,8 @@
     attend(0, 2 * ROWS, True)
 
     inner[0].wait_send()
-    inner[1].start()
+    outer[0].start()
+    outer[2].start()
     passes = []
     for i in range(3):
         for copy in ([inner[i]] if i < 2 else [outer[0], outer[2]]):
@@ -291,10 +293,6 @@
         onward = remote(far.at[2 * i], far.at[2 * i + 1], 9 + i, sibling)
         onward.start()
         passes.append(onward)
-        if i == 0:
-            inner[1].wait_send()
-            outer[0].start()
-            outer[2].start()
         onward.wait_recv()
         place = 2 * ROWS + 2 * CHUNK * i
         keys_values(far[2 * i : 2 * i + 2].reshape(2 * CHUNK, C), place, 2 * CHUNK)
@@ -304,7 +302,7 @@
         parts = []
         for j in range(2):
             p = 2 * g + j
-            both = acc[p] / acc[p, :, 192 * (1 - j) : 192 * (1 - j) + 1]
+            both = acc[p] * (1.0 / acc[p, :, 192 * (1 - j) : 192 * (1 - j) + 1])
             first = j * 64
             one = (lane >= first) & (lane < first + 96)
             two = (lane >= first + 96) & (lane < first + 192)
@@ -355,12 +353,12 @@
     def _():
         to_right.wait_send()
 
-    for copy in [inner_near] + outer + passes + shares:
+    for copy in [inner[1], inner_near] + outer + passes + shares:
         copy.wait_send()
 
 
-def finale(track_hbm, left_ref, rights_ref, track_out, pair_ref, sem):
-    copy = pltpu.make_async_copy(track_hbm, track_out, sem)
+def finale(track_ref, left_ref, rights_ref, track_out, pair_ref, sem):
+    copy = pltpu.make_async_copy(track_ref, track_out, sem)
     copy.start()
     left = left_ref[...].astype(F32)
     channel = lax.rem(lax.broadcasted_iota(jnp.int32, (PCH, 1, R * PCH), 2), PCH)
@@ -422,7 +420,7 @@
             jax.ShapeDtypeStruct((ROWS, C), BF),
             jax.ShapeDtypeStruct((PCH, ROWS // POOL, GROUP * ROWS // POOL), BF),
         ),
-        in_specs=[hbm, vmem, vmem],
+        in_specs=[vmem, vmem, vmem],
         out_specs=(hbm, vmem),
         scratch_shapes=[pltpu.SemaphoreType.DMA],
     )(track, left, rights)

time: 99.6 us -> 79.6 us (0.80)
  Pallas kernels: 98.6 us -> 78.6 us
    pallas_call x1, Pallas kernels: 20.6 us -> 2.66 us  [body(): pl.pallas_call(finale, out_shape=(jax.ShapeDtypeStruct((ROWS, C), BF), ja...]
    pallas_call x1, Pallas kernels: 77.9 us -> 76 us  [body(): pl.pallas_call(kernel, out_shape=(jax.ShapeDtypeStruct((ROWS, C), BF), ja...]
where the time goes in v3:
time: 79.6 us; the launch traced here: 79.4 us
  Pallas kernels  78.6 us (99%)
  between operations  0.8 us (1%)
    pallas_call x1, Pallas kernels, body(): pl.pallas_call(kernel, out_shape=(jax.ShapeDtypeStruct((ROWS, C), BF), ja...  76 us
    pallas_call x1, Pallas kernels, body(): pl.pallas_call(finale, out_shape=(jax.ShapeDtypeStruct((ROWS, C), BF), ja...  2.66 us

profile of v3, /device:TPU:311, one launch (start us, length us, event | category | flops | bytes accessed | tf_op | source)
XLA Modules:
  0.0 79.4 jit_solution(12763609929149294150)
XLA Ops:
  0.6 76.0 %shard_map.104 = (bf16[384,768]{1,0:T(8,128)(2,1)}, bf16[24,512]{1,0:T(8,128)(2,1)}, bf16[4,24,512]{2,1,0:T(8,128)(2,1)}) custom-call(bf16[384,768]{1,0:T(8,128)(2,1)} %x_ref.1, f32[4,768]{1,0:T(4,128)} %gain_ref.1, f32[5,4,768]{2,1,0:T(4,128)} %bitcast.1, s32[4]{0:T(128)} %dil_ref.1, f32[768]{0:T(1024)} %again_ref.1, bf16[768,2304]{1,0:T(8,128)(2,1)} %wqkv_hbm.1, ...), custom_call_target="tpu_custom_call" | custom-call | tf_op jit(solution)/shard_map/pallas_call | solution.py:381
  76.6 2.7 %shard_map.105 = (bf16[384,768]{1,0:T(8,128)(2,1)}, bf16[64,24,96]{2,1,0:T(8,128)(2,1)}) custom-call(bf16[384,768]{1,0:T(8,128)(2,1)} %get-tuple-element.5.track_ref, bf16[24,512]{1,0:T(8,128)(2,1)} %get-tuple-element.6.left_ref, bf16[4,24,512]{2,1,0:T(8,128)(2,1)} %get-tuple-element.7.rights_ref), custom_call_target="tpu_custom_call" | custom-call | tf_op jit(solution)/shard_map/pallas_call | solution.py:417

commit v4 on v3

--- a/solution.py
+++ b/solution.py
@@ -28,12 +28,12 @@
 BF = jnp.bfloat16
 F32 = jnp.float32
 MESH = pl.DeviceIdType.MESH
+ROOT = math.sqrt(2 / math.pi)
 LOG2E = math.log2(math.e)
 
 
-def gelu(v):
-    u = v * (math.sqrt(2 / math.pi) + math.sqrt(2 / math.pi) * 0.044715 * (v * v))
-    half = 0.5 * v
+def gelu_of_double(half):
+    u = half * (2 * ROOT + 8 * 0.044715 * ROOT * (half * half))
     return half + half * jnp.tanh(u)
 
 
@@ -80,7 +80,7 @@
                 total = taps[0] * hbuf[c, pl.ds(q + REACH - 2 * d, STEP)]
                 for t in range(1, KSIZE):
                     total = total + taps[t] * hbuf[c, pl.ds(q + REACH + (t - 2) * d, STEP)]
-                seg[c, q : q + STEP] = seg[c, q : q + STEP] + gelu(total)
+                seg[c, q : q + STEP] = seg[c, q : q + STEP] + gelu_of_double(total)
         return 0
 
     lax.fori_loop(0, LAYERS, layer, 0)
@@ -125,8 +125,31 @@
     for target in (sibling, partner, cross):
         pl.semaphore_signal(barrier, inc=1, device_id={"seq": target}, device_id_type=MESH)
 
+    to_left = remote(x_ref.at[pl.ds(0, EDGE)], halo.at[1], 0, lax.rem(block + GROUP - 1, GROUP))
+    to_right = remote(
+        x_ref.at[pl.ds(ROWS - EDGE, EDGE)], halo.at[0], 1, lax.rem(block + 1, GROUP)
+    )
+    has_left, has_right = block > 0, block < GROUP - 1
+
+    upper = block >= GROUP // 2
+
+    def meet():
+        pl.semaphore_wait(barrier, 3)
+
+        @pl.when(has_left)
+        def _():
+            to_left.start()
+
+        @pl.when(has_right)
+        def _():
+            to_right.start()
+
+    @pl.when(upper)
+    def _():
+        meet()
+
     for t in range(KSIZE):
-        product = taps_ref[t] * gain_ref[...]
+        product = (taps_ref[t] * gain_ref[...]) * 0.5
         for l in range(LAYERS):
             scaled[l, t : t + 1] = product[l : l + 1]
     for c in range(CT):
@@ -148,21 +171,9 @@
 
     for start in range(EDGE, ROWS - EDGE, 64):
         finish(start, start, 64)
-    pl.semaphore_wait(barrier, 3)
-
-    to_left = remote(x_ref.at[pl.ds(0, EDGE)], halo.at[1], 0, lax.rem(block + GROUP - 1, GROUP))
-    to_right = remote(
-        x_ref.at[pl.ds(ROWS - EDGE, EDGE)], halo.at[0], 1, lax.rem(block + 1, GROUP)
-    )
-    has_left, has_right = block > 0, block < GROUP - 1
-
-    @pl.when(has_left)
-    def _():
-        to_left.start()
-
-    @pl.when(has_right)
-    def _():
-        to_right.start()
+    @pl.when(jnp.logical_not(upper))
+    def _():
+        meet()
 
     inner = [
         remote(near.at[0, pl.ds(EDGE + i * CHUNK, CHUNK)], far.at[2 * i], 2 + i, partner)
@@ -208,8 +219,8 @@
         rows = pl.ds(start, EDGE)
         outer.append(remote(near.at[0, rows], far.at[4, pl.ds(i * EDGE, EDGE)], 4 + i, partner))
         outer.append(remote(near.at[0, rows], near.at[1, rows], 7 + i, sibling))
-    outer[1].start()
-    outer[3].start()
+    for copy in outer:
+        copy.start()
 
     weights[0].wait()
 
@@ -283,19 +294,21 @@
     keys_values(near[...].reshape(2 * ROWS, C), 0, 2 * ROWS)
     attend(0, 2 * ROWS, True)
 
-    inner[0].wait_send()
-    outer[0].start()
-    outer[2].start()
     passes = []
     for i in range(3):
+        place = 2 * ROWS + 2 * CHUNK * i
+        onward = remote(far.at[2 * i], far.at[2 * i + 1], 9 + i, sibling)
         for copy in ([inner[i]] if i < 2 else [outer[0], outer[2]]):
             copy.wait_recv()
-        onward = remote(far.at[2 * i], far.at[2 * i + 1], 9 + i, sibling)
         onward.start()
         passes.append(onward)
-        onward.wait_recv()
-        place = 2 * ROWS + 2 * CHUNK * i
-        keys_values(far[2 * i : 2 * i + 2].reshape(2 * CHUNK, C), place, 2 * CHUNK)
+        if i < 2:
+            onward.wait_recv()
+            keys_values(far[2 * i : 2 * i + 2].reshape(2 * CHUNK, C), place, 2 * CHUNK)
+        else:
+            keys_values(far[2 * i], place, CHUNK)
+            onward.wait_recv()
+            keys_values(far[2 * i + 1], place + CHUNK, CHUNK)
         attend(place, 2 * CHUNK, False)
 
     for g in range(2):
@@ -353,7 +366,7 @@
     def _():
         to_right.wait_send()
 
-    for copy in [inner[1], inner_near] + outer + passes + shares:
+    for copy in inner + [inner_near] + outer + passes + shares:
         copy.wait_send()
 
 

time: 79.6 us -> 75.6 us (0.950)
  Pallas kernels: 78.6 us -> 74.6 us
    pallas_call x1, Pallas kernels: 76 us -> 71.9 us  [body(): pl.pallas_call(kernel, out_shape=(jax.ShapeDtypeStruct((ROWS, C), BF), ja...]
where the time goes in v4:
time: 75.6 us; the launch traced here: 75.4 us
  Pallas kernels  74.6 us (99%)
  between operations  0.82 us (1%)
    pallas_call x1, Pallas kernels, body(): pl.pallas_call(kernel, out_shape=(jax.ShapeDtypeStruct((ROWS, C), BF), ja...  71.9 us
    pallas_call x1, Pallas kernels, body(): pl.pallas_call(finale, out_shape=(jax.ShapeDtypeStruct((ROWS, C), BF), ja...  2.66 us

profile of v4, /device:TPU:311, one launch (start us, length us, event | category | flops | bytes accessed | tf_op | source)
XLA Modules:
  0.0 75.4 jit_solution(512956306241387542)
XLA Ops:
  0.6 71.9 %shard_map.104 = (bf16[384,768]{1,0:T(8,128)(2,1)}, bf16[24,512]{1,0:T(8,128)(2,1)}, bf16[4,24,512]{2,1,0:T(8,128)(2,1)}) custom-call(bf16[384,768]{1,0:T(8,128)(2,1)} %x_ref.1, f32[4,768]{1,0:T(4,128)} %gain_ref.1, f32[5,4,768]{2,1,0:T(4,128)} %bitcast.1, s32[4]{0:T(128)} %dil_ref.1, f32[768]{0:T(1024)} %again_ref.1, bf16[768,2304]{1,0:T(8,128)(2,1)} %wqkv_hbm.1, ...), custom_call_target="tpu_custom_call" | custom-call | tf_op jit(solution)/shard_map/pallas_call | solution.py:394
  72.6 2.7 %shard_map.105 = (bf16[384,768]{1,0:T(8,128)(2,1)}, bf16[64,24,96]{2,1,0:T(8,128)(2,1)}) custom-call(bf16[384,768]{1,0:T(8,128)(2,1)} %get-tuple-element.5.track_ref, bf16[24,512]{1,0:T(8,128)(2,1)} %get-tuple-element.6.left_ref, bf16[4,24,512]{2,1,0:T(8,128)(2,1)} %get-tuple-element.7.rights_ref), custom_call_target="tpu_custom_call" | custom-call | tf_op jit(solution)/shard_map/pallas_call | solution.py:430

commit v5 on v4

--- a/solution.py
+++ b/solution.py
@@ -169,22 +169,28 @@
                 rows[c] * scale * again_ref[cols][None]
             ).astype(BF)
 
-    for start in range(EDGE, ROWS - EDGE, 64):
+    for start in range(EDGE, EDGE + CHUNK, 64):
         finish(start, start, 64)
+
     @pl.when(jnp.logical_not(upper))
     def _():
         meet()
 
     inner = [
-        remote(near.at[0, pl.ds(EDGE + i * CHUNK, CHUNK)], far.at[2 * i], 2 + i, partner)
+        remote(
+            near.at[0, pl.ds(EDGE + i * CHUNK, CHUNK)], far.at[0, pl.ds(i * CHUNK, CHUNK)],
+            2 + i, partner,
+        )
         for i in range(2)
     ]
+    inner[0].start()
+    for start in range(EDGE + CHUNK, ROWS - EDGE, 64):
+        finish(start, start, 64)
+    inner[1].start()
     inner_near = remote(
         near.at[0, pl.ds(EDGE, 2 * CHUNK)], near.at[1, pl.ds(EDGE, 2 * CHUNK)], 6, sibling
     )
     inner_near.start()
-    inner[0].start()
-    inner[1].start()
 
     @pl.when(has_left)
     def _():
@@ -217,7 +223,11 @@
     outer = []
     for i, start in enumerate((0, ROWS - EDGE)):
         rows = pl.ds(start, EDGE)
-        outer.append(remote(near.at[0, rows], far.at[4, pl.ds(i * EDGE, EDGE)], 4 + i, partner))
+        outer.append(
+            remote(
+                near.at[0, rows], far.at[0, pl.ds(2 * CHUNK + i * EDGE, EDGE)], 4 + i, partner
+            )
+        )
         outer.append(remote(near.at[0, rows], near.at[1, rows], 7 + i, sibling))
     for copy in outer:
         copy.start()
@@ -295,33 +305,63 @@
     attend(0, 2 * ROWS, True)
 
     passes = []
-    for i in range(3):
-        place = 2 * ROWS + 2 * CHUNK * i
-        onward = remote(far.at[2 * i], far.at[2 * i + 1], 9 + i, sibling)
-        for copy in ([inner[i]] if i < 2 else [outer[0], outer[2]]):
-            copy.wait_recv()
+
+    def pass_on(first, count, index):
+        rows = pl.ds(first, count)
+        onward = remote(far.at[0, rows], far.at[1, rows], index, sibling)
         onward.start()
         passes.append(onward)
-        if i < 2:
-            onward.wait_recv()
-            keys_values(far[2 * i : 2 * i + 2].reshape(2 * CHUNK, C), place, 2 * CHUNK)
-        else:
-            keys_values(far[2 * i], place, CHUNK)
-            onward.wait_recv()
-            keys_values(far[2 * i + 1], place + CHUNK, CHUNK)
-        attend(place, 2 * CHUNK, False)
+        return onward
+
+    inner[0].wait_recv()
+    pass_on(0, CHUNK, 9).wait_recv()
+    keys_values(far[:, :CHUNK].reshape(2 * CHUNK, C), 2 * ROWS, 2 * CHUNK)
+    attend(2 * ROWS, 2 * CHUNK, False)
+    inner[1].wait_recv()
+    second = pass_on(CHUNK, CHUNK, 10)
+    outer[0].wait_recv()
+    third = pass_on(2 * CHUNK, EDGE, 11)
+    second.wait_recv()
+    third.wait_recv()
+    count = CHUNK + EDGE
+    place = 2 * ROWS + 2 * CHUNK
+    keys_values(far[:, CHUNK : CHUNK + count].reshape(2 * count, C), place, 2 * count)
+    attend(place, 2 * count, False)
+    place = place + 2 * count
+    outer[2].wait_recv()
+    last = pass_on(ROWS - EDGE, EDGE, 12)
+    keys_values(far[0, ROWS - EDGE :], place, EDGE)
+    last.wait_recv()
+    keys_values(far[1, ROWS - EDGE :], place + EDGE, EDGE)
 
     for g in range(2):
         parts = []
         for j in range(2):
             p = 2 * g + j
-            both = acc[p] * (1.0 / acc[p, :, 192 * (1 - j) : 192 * (1 - j) + 1])
+            cols = slice(window(p), window(p) + WIN)
+            means = []
+            for i in range(2):
+                rows = slice(i * ROWS, (i + 1) * ROWS)
+                scores = lax.dot_general(
+                    q2[p, rows], keys[place:, cols],
+                    (((1,), (1,)), ((), ())), preferred_element_type=F32,
+                )
+                old = top[p, rows]
+                peak = jnp.maximum(old, jnp.max(scores, axis=-1, keepdims=True))
+                probs = jnp.exp2((scores - peak) * SCALE).astype(BF)
+                rescale = jnp.exp2((old - peak) * SCALE)
+                out = jnp.dot(probs, values[p, place:], preferred_element_type=F32)
+                total = [
+                    acc[p, rows, k : k + LANES] * rescale + out[:, k : k + LANES]
+                    for k in range(0, WIN, LANES)
+                ]
+                ones = total[1][:, 64:65] if j == 0 else total[0][:, 0:1]
+                weight = 1.0 / ones
+                means.append(jnp.concatenate([half * weight for half in total], axis=1))
             first = j * 64
             one = (lane >= first) & (lane < first + 96)
             two = (lane >= first + 96) & (lane < first + 192)
-            parts.append(
-                jnp.where(one, both[:ROWS], jnp.where(two, both[ROWS:], 0.0))
-            )
+            parts.append(jnp.where(one, means[0], jnp.where(two, means[1], 0.0)))
         base = g * 3 * LANES
         mixed[:, base : base + LANES] = parts[0][:, :LANES].astype(BF)
         mixed[:, base + LANES : base + 2 * LANES] = (
@@ -349,7 +389,7 @@
     right = jnp.dot(pooled, wb[...], preferred_element_type=F32).astype(BF)
     rights[pl.ds(block, 1)] = right[None]
     shares = [
-        remote(rights.at[block], rights.at[block], 12 + i, target)
+        remote(rights.at[block], rights.at[block], 13 + i, target)
         for i, target in enumerate((sibling, partner, cross))
     ]
     for copy in shares[::-1]:
@@ -394,9 +434,9 @@
     track, left, rights = pl.pallas_call(
         kernel,
         out_shape=(
-            jax.ShapeDtypeStruct((ROWS, C), BF),
-            jax.ShapeDtypeStruct((ROWS // POOL, R * PCH), BF),
-            jax.ShapeDtypeStruct((GROUP, ROWS // POOL, R * PCH), BF),
+            pltpu.VMEM((ROWS, C), BF),
+            pltpu.VMEM((ROWS // POOL, R * PCH), BF),
+            pltpu.VMEM((GROUP, ROWS // POOL, R * PCH), BF),
         ),
         in_specs=[vmem, vmem, vmem, pl.BlockSpec(memory_space=pltpu.SMEM), vmem, hbm, hbm, hbm, hbm],
         out_specs=(vmem, vmem, vmem),
@@ -412,7 +452,7 @@
             pltpu.VMEM((CT, ROWS, LANES), F32),
             pltpu.VMEM((2, EDGE, C), BF),
             pltpu.VMEM((2, ROWS, C), BF),
-            pltpu.VMEM((6, CHUNK, C), BF),
+            pltpu.VMEM((2, ROWS, C), BF),
             pltpu.VMEM((GROUP * ROWS, C), BF),
             pltpu.VMEM((PAIRS, GROUP * ROWS, WIN), BF),
             pltpu.VMEM((PAIRS, 2 * ROWS, WIN), BF),
@@ -420,8 +460,8 @@
             pltpu.VMEM((PAIRS, 2 * ROWS, WIN), F32),
             pltpu.VMEM((ROWS, C), BF),
             pltpu.SemaphoreType.DMA((4,)),
-            pltpu.SemaphoreType.DMA((15,)),
-            pltpu.SemaphoreType.DMA((15,)),
+            pltpu.SemaphoreType.DMA((16,)),
+            pltpu.SemaphoreType.DMA((16,)),
         ],
         compiler_params=pltpu.CompilerParams(
             collective_id=0, has_side_effects=True, vmem_limit_bytes=60 * 1024 * 1024
@@ -436,7 +476,7 @@
         in_specs=[vmem, vmem, vmem],
         out_specs=(hbm, vmem),
         scratch_shapes=[pltpu.SemaphoreType.DMA],
-    )(track, left, rights)
+    )(*[pltpu.with_memory_space_constraint(v, pltpu.VMEM) for v in (track, left, rights)])
 
 
 def solution(mesh):

time: 75.6 us -> 77.2 us (1.021)
  the two profiles are of different devices: /device:TPU:311 before, /device:TPU:299 now
where the time goes in v5:
time: 77.2 us; the launch traced here: 77 us
  Pallas kernels  76.2 us (99%)
  between operations  0.82 us (1%)
    pallas_call x1, Pallas kernels, body(): pl.pallas_call(kernel, out_shape=(pltpu.VMEM((ROWS, C), BF), pltpu.VMEM((...  74.6 us
    pallas_call x1, Pallas kernels, body(): pl.pallas_call(finale, out_shape=(jax.ShapeDtypeStruct((ROWS, C), BF), ja...  1.64 us

profile of v5, /device:TPU:299, one launch (start us, length us, event | category | flops | bytes accessed | tf_op | source)
XLA Modules:
  0.0 77.0 jit_solution(6798449575365289279)
XLA Ops:
  0.6 74.6 %shard_map.104 = (bf16[384,768]{1,0:T(8,128)(2,1)S(1)}, bf16[24,512]{1,0:T(8,128)(2,1)S(1)}, bf16[4,24,512]{2,1,0:T(8,128)(2,1)S(1)}) custom-call(bf16[384,768]{1,0:T(8,128)(2,1)} %x_ref.1, f32[4,768]{1,0:T(4,128)} %gain_ref.1, f32[5,4,768]{2,1,0:T(4,128)} %bitcast.1, s32[4]{0:T(128)} %dil_ref.1, f32[768]{0:T(1024)} %again_ref.1, ...), custom_call_target="tpu_custom_call" | custom-call | tf_op jit(solution)/shard_map/pallas_call | solution.py:434
  75.2 1.6 %shard_map.105 = (bf16[384,768]{1,0:T(8,128)(2,1)}, bf16[64,24,96]{2,1,0:T(8,128)(2,1)}) custom-call(bf16[384,768]{1,0:T(8,128)(2,1)S(1)} %get-tuple-element.5.track_ref, bf16[24,512]{1,0:T(8,128)(2,1)S(1)} %get-tuple-element.6.left_ref, bf16[4,24,512]{2,1,0:T(8,128)(2,1)S(1)} %get-tuple-element.7.rights_ref), custom_call_target="tpu_custom_call" | custom-call | tf_op jit(solution)/shard_map/pallas_call | solution.py:470

commit v6 on v5

--- a/solution.py
+++ b/solution.py
@@ -318,21 +318,18 @@
     keys_values(far[:, :CHUNK].reshape(2 * CHUNK, C), 2 * ROWS, 2 * CHUNK)
     attend(2 * ROWS, 2 * CHUNK, False)
     inner[1].wait_recv()
-    second = pass_on(CHUNK, CHUNK, 10)
+    pass_on(CHUNK, CHUNK, 10).wait_recv()
+    keys_values(far[:, CHUNK : 2 * CHUNK].reshape(2 * CHUNK, C), 2 * ROWS + 2 * CHUNK, 2 * CHUNK)
+    attend(2 * ROWS + 2 * CHUNK, 2 * CHUNK, False)
+    place = 2 * ROWS + 4 * CHUNK
     outer[0].wait_recv()
-    third = pass_on(2 * CHUNK, EDGE, 11)
-    second.wait_recv()
-    third.wait_recv()
-    count = CHUNK + EDGE
-    place = 2 * ROWS + 2 * CHUNK
-    keys_values(far[:, CHUNK : CHUNK + count].reshape(2 * count, C), place, 2 * count)
-    attend(place, 2 * count, False)
-    place = place + 2 * count
+    last = [pass_on(2 * CHUNK, EDGE, 11)]
     outer[2].wait_recv()
-    last = pass_on(ROWS - EDGE, EDGE, 12)
-    keys_values(far[0, ROWS - EDGE :], place, EDGE)
-    last.wait_recv()
-    keys_values(far[1, ROWS - EDGE :], place + EDGE, EDGE)
+    last.append(pass_on(2 * CHUNK + EDGE, EDGE, 12))
+    keys_values(far[0, 2 * CHUNK :], place, CHUNK)
+    for copy in last:
+        copy.wait_recv()
+    keys_values(far[1, 2 * CHUNK :], place + CHUNK, CHUNK)
 
     for g in range(2):
         parts = []
@@ -347,8 +344,12 @@
                     (((1,), (1,)), ((), ())), preferred_element_type=F32,
                 )
                 old = top[p, rows]
-                peak = jnp.maximum(old, jnp.max(scores, axis=-1, keepdims=True))
-                probs = jnp.exp2((scores - peak) * SCALE).astype(BF)
+                pieces = [scores[:, k : k + LANES] for k in range(0, 2 * CHUNK, LANES)]
+                peak = jnp.max(jnp.maximum(*pieces), axis=-1, keepdims=True)
+                peak = jnp.maximum(old, peak)
+                probs = jnp.concatenate(
+                    [jnp.exp2((piece - peak) * SCALE).astype(BF) for piece in pieces], axis=1
+                )
                 rescale = jnp.exp2((old - peak) * SCALE)
                 out = jnp.dot(probs, values[p, place:], preferred_element_type=F32)
                 total = [

time: 77.2 us -> 73.8 us (0.956)
  the two profiles are of different devices: /device:TPU:299 before, /device:TPU:317 now
where the time goes in v6:
time: 73.8 us; the launch traced here: 73.7 us
  Pallas kernels  72.8 us (99%)
  between operations  0.82 us (1%)
    pallas_call x1, Pallas kernels, body(): pl.pallas_call(kernel, out_shape=(pltpu.VMEM((ROWS, C), BF), pltpu.VMEM((...  71.2 us
    pallas_call x1, Pallas kernels, body(): pl.pallas_call(finale, out_shape=(jax.ShapeDtypeStruct((ROWS, C), BF), ja...  1.64 us

profile of v6, /device:TPU:317, one launch (start us, length us, event | category | flops | bytes accessed | tf_op | source)
XLA Modules:
  0.0 73.7 jit_solution(10003015013461337493)
XLA Ops:
  0.6 71.2 %shard_map.104 = (bf16[384,768]{1,0:T(8,128)(2,1)S(1)}, bf16[24,512]{1,0:T(8,128)(2,1)S(1)}, bf16[4,24,512]{2,1,0:T(8,128)(2,1)S(1)}) custom-call(bf16[384,768]{1,0:T(8,128)(2,1)} %x_ref.1, f32[4,768]{1,0:T(4,128)} %gain_ref.1, f32[5,4,768]{2,1,0:T(4,128)} %bitcast.1, s32[4]{0:T(128)} %dil_ref.1, f32[768]{0:T(1024)} %again_ref.1, ...), custom_call_target="tpu_custom_call" | custom-call | tf_op jit(solution)/shard_map/pallas_call | solution.py:435
  71.8 1.6 %shard_map.105 = (bf16[384,768]{1,0:T(8,128)(2,1)}, bf16[64,24,96]{2,1,0:T(8,128)(2,1)}) custom-call(bf16[384,768]{1,0:T(8,128)(2,1)S(1)} %get-tuple-element.5.track_ref, bf16[24,512]{1,0:T(8,128)(2,1)S(1)} %get-tuple-element.6.left_ref, bf16[4,24,512]{2,1,0:T(8,128)(2,1)S(1)} %get-tuple-element.7.rights_ref), custom_call_target="tpu_custom_call" | custom-call | tf_op jit(solution)/shard_map/pallas_call | solution.py:471

commit v7 on v6

--- a/solution.py
+++ b/solution.py
@@ -97,7 +97,7 @@
 
 def kernel(
     x_ref, gain_ref, taps_ref, dil_ref, again_ref, wqkv_hbm, wout_hbm, wa_hbm, wb_hbm,
-    track_ref, left_ref, rights,
+    track_ref, spread_ref, rights,
     wqkv, wout, wa, wb, scaled, nat, seg, hbuf, state, halo, near, far, keys, values, q2,
     top, acc, mixed, wsem, send, recv,
 ):
@@ -380,7 +380,7 @@
         for j in range(WIN // LANES):
             c = t * (WIN // LANES) + j
             result = state[c] + product[:, j * LANES : (j + 1) * LANES]
-            track_ref[:, c * LANES : (c + 1) * LANES] = result.astype(BF)
+            state[c] = result
             pool = jnp.sum(result.reshape(ROWS // POOL, POOL, LANES), axis=1) * (1.0 / POOL)
             squares = squares + pool * pool
             pools.append(pool)
@@ -395,8 +395,14 @@
     ]
     for copy in shares[::-1]:
         copy.start()
+    for c in range(CT):
+        track_ref[:, c * LANES : (c + 1) * LANES] = state[c].astype(BF)
     weights[2].wait()
-    left_ref[...] = jnp.dot(pooled, wa[...], preferred_element_type=F32).astype(BF)
+    left = jnp.dot(pooled, wa[...], preferred_element_type=F32).astype(BF).astype(F32)
+    channel = lax.rem(lax.broadcasted_iota(jnp.int32, (PCH, 1, R * PCH), 2), PCH)
+    wanted = lax.broadcasted_iota(jnp.int32, (PCH, 1, R * PCH), 0)
+    spread = jnp.where(channel == wanted, left[None], 0.0)
+    spread_ref[...] = spread.reshape(PCH * (ROWS // POOL), R * PCH).astype(BF)
     for copy in shares:
         copy.wait_recv()
     @pl.when(has_left)
@@ -411,17 +417,12 @@
         copy.wait_send()
 
 
-def finale(track_ref, left_ref, rights_ref, track_out, pair_ref, sem):
+def finale(track_ref, spread_ref, rights_ref, track_out, pair_ref, sem):
     copy = pltpu.make_async_copy(track_ref, track_out, sem)
     copy.start()
-    left = left_ref[...].astype(F32)
-    channel = lax.rem(lax.broadcasted_iota(jnp.int32, (PCH, 1, R * PCH), 2), PCH)
-    wanted = lax.broadcasted_iota(jnp.int32, (PCH, 1, R * PCH), 0)
-    spread = jnp.where(channel == wanted, left[None], 0.0)
-    spread = spread.reshape(PCH * (ROWS // POOL), R * PCH).astype(BF)
     every = jnp.concatenate([rights_ref[i].astype(F32) for i in range(GROUP)], axis=0).astype(BF)
     product = lax.dot_general(
-        spread, every, (((1,), (1,)), ((), ())), preferred_element_type=F32
+        spread_ref[...], every, (((1,), (1,)), ((), ())), preferred_element_type=F32
     )
     pair_ref[...] = (
         (product * (1.0 / math.sqrt(R))).reshape(PCH, ROWS // POOL, GROUP * ROWS // POOL)
@@ -432,11 +433,11 @@
 def body(x, conv_gain, conv_kernel, dilation, attn_gain, w_qkv, w_out, w_pair_a, w_pair_b):
     vmem = pl.BlockSpec(memory_space=pltpu.VMEM)
     hbm = pl.BlockSpec(memory_space=pl.ANY)
-    track, left, rights = pl.pallas_call(
+    track, spread, rights = pl.pallas_call(
         kernel,
         out_shape=(
             pltpu.VMEM((ROWS, C), BF),
-            pltpu.VMEM((ROWS // POOL, R * PCH), BF),
+            pltpu.VMEM((PCH * (ROWS // POOL), R * PCH), BF),
             pltpu.VMEM((GROUP, ROWS // POOL, R * PCH), BF),
         ),
         in_specs=[vmem, vmem, vmem, pl.BlockSpec(memory_space=pltpu.SMEM), vmem, hbm, hbm, hbm, hbm],
@@ -477,7 +478,8 @@
         in_specs=[vmem, vmem, vmem],
         out_specs=(hbm, vmem),
         scratch_shapes=[pltpu.SemaphoreType.DMA],
-    )(*[pltpu.with_memory_space_constraint(v, pltpu.VMEM) for v in (track, left, rights)])
+        compiler_params=pltpu.CompilerParams(vmem_limit_bytes=32 * 1024 * 1024),
+    )(*[pltpu.with_memory_space_constraint(v, pltpu.VMEM) for v in (track, spread, rights)])
 
 
 def solution(mesh):

time: 73.8 us -> 73.9 us (level)
  the two profiles are of different devices: /device:TPU:317 before, /device:TPU:313 now
where the time goes in v7:
time: 73.9 us; the launch traced here: 73.7 us
  Pallas kernels  72.9 us (99%)
  between operations  0.82 us (1%)
    pallas_call x1, Pallas kernels, body(): pl.pallas_call(kernel, out_shape=(pltpu.VMEM((ROWS, C), BF), pltpu.VMEM((...  71.2 us
    pallas_call x1, Pallas kernels, body(): pl.pallas_call(finale, out_shape=(jax.ShapeDtypeStruct((ROWS, C), BF), ja...  1.69 us

profile of v7, /device:TPU:313, one launch (start us, length us, event | category | flops | bytes accessed | tf_op | source)
XLA Modules:
  0.0 73.7 jit_solution(10479385965052342821)
XLA Ops:
  0.6 71.2 %shard_map.104 = (bf16[384,768]{1,0:T(8,128)(2,1)S(1)}, bf16[1536,512]{1,0:T(8,128)(2,1)S(1)}, bf16[4,24,512]{2,1,0:T(8,128)(2,1)S(1)}) custom-call(bf16[384,768]{1,0:T(8,128)(2,1)} %x_ref.1, f32[4,768]{1,0:T(4,128)} %gain_ref.1, f32[5,4,768]{2,1,0:T(4,128)} %bitcast.1, s32[4]{0:T(128)} %dil_ref.1, f32[768]{0:T(1024)} %again_ref.1, ...), custom_call_target="tpu_custom_call" | custom-call | tf_op jit(solution)/shard_map/pallas_call | solution.py:436
  71.8 1.7 %shard_map.105 = (bf16[384,768]{1,0:T(8,128)(2,1)}, bf16[64,24,96]{2,1,0:T(8,128)(2,1)}) custom-call(bf16[384,768]{1,0:T(8,128)(2,1)S(1)} %get-tuple-element.5.track_ref, bf16[1536,512]{1,0:T(8,128)(2,1)S(1)} %get-tuple-element.6.spread_ref, bf16[4,24,512]{2,1,0:T(8,128)(2,1)S(1)} %get-tuple-element.7.rights_ref), custom_call_target="tpu_custom_call" | custom-call | tf_op jit(solution)/shard_map/pallas_call | solution.py:472
